TPU v7x, 32 devices: a whole 2x2x4 slice. The times are simulated.
32 devices in a mesh: blk: 8 (over y, x, core), feat: 4 (over z).
Axes of the slice: x: 2, y: 2, z: 4, core: 2. Of those that a mesh axis runs over, the one named last changes fastest.
Arguments:
- features: bfloat16 [24576, 512], P('blk', 'feat'), may hold values from -6 to 6
- tile_values: bfloat16 [1024, 128, 128], P('blk'), may hold values from -0.375 to 0.375
- tile_rows: int32 [1024], P('blk'), may hold values from 0 to 23, as said below
- tile_cols: int32 [1024], P('blk'), may hold values from 0 to 23, as said below
- tile_counts: int32 [64], P('blk'), may hold values from 1 to 16, as said below
- weight: bfloat16 [512, 512], replicated, may hold values from -0.25 to 0.25
- bias: float32 [512], P('feat'), may hold values from -3 to 3
Outputs:
- hidden: bfloat16 [24576, 512], P('blk', 'feat')
Inputs may be any that keep to these rules, and one draw needn't show every extreme that they name: `tile_rows`: the live slots of one node block and offset name distinct pairs of row and column tiles. `tile_cols`: paired with tile_rows slot by slot. `tile_counts`: some block and offset has all 16 slots live in every draw.
All inputs are finite; a program needn't handle non-finite values.
Results may differ from a plain program's by a relative error of at most 0.0049.
Values may be sent and summed in bfloat16 or wider, within the bound.
No kernel may reach another device: no remote copies, remote signals or barrier semaphores. Data moves between devices by JAX's collectives and lax.ppermute only.
A program may use at most 64 MiB of HBM per device.

v0:
```python
import jax
import jax.numpy as jnp
from jax import lax
from jax.sharding import PartitionSpec as P


def shifted(shard, axis, by):
    count = lax.axis_size(axis)
    return lax.ppermute(shard, axis, [(i, (i + by) % count) for i in range(count)])


def pick_tiles(current, wanted, row_tiles, tile_size):
    source = current.reshape(row_tiles, tile_size, current.shape[-1])
    return jnp.take(source, wanted, axis=0)


def add_tiles(totals, picked, offset, values_all, row_ids, tile_counts):
    row_tiles = totals.shape[0]
    slot_count = row_ids.shape[1]
    products = jnp.einsum(
        "ktj,kjf->ktf", values_all[offset], picked, preferred_element_type=jnp.float32
    )
    active = jnp.arange(slot_count) < tile_counts[offset]
    one_hot = (
        (row_ids[offset][None, :] == jnp.arange(row_tiles)[:, None]) & active[None, :]
    ).astype(jnp.float32)
    return totals + jnp.einsum("rk,ktf->rtf", one_hot, products, precision=lax.Precision.HIGHEST)


def body(features, tile_values, tile_rows, tile_cols, tile_counts, weight, bias):
    row_count, col_width = features.shape
    tile_size = tile_values.shape[-1]
    row_tiles = row_count // tile_size
    steps_all = tile_counts.shape[0]
    slot_count = tile_rows.shape[0] // steps_all
    values_all = tile_values.reshape(steps_all, slot_count, tile_size, tile_size)
    row_ids = tile_rows.reshape(steps_all, slot_count)
    col_ids = tile_cols.reshape(steps_all, slot_count)
    totals = jnp.zeros((row_tiles, tile_size, col_width), jnp.float32)
    own_picked = pick_tiles(features, col_ids[0], row_tiles, tile_size)
    totals = add_tiles(totals, own_picked, 0, values_all, row_ids, tile_counts)
    current = features
    for offset in range(1, steps_all):
        current = shifted(current, "blk", 1)
        picked = pick_tiles(current, col_ids[offset], row_tiles, tile_size)
        totals = add_tiles(totals, picked, offset, values_all, row_ids, tile_counts)
    aggregate = totals.reshape(row_count, col_width).astype(jnp.bfloat16)
    out_width = bias.shape[0]
    member = lax.axis_index("feat")
    own_cols = lax.dynamic_slice_in_dim(weight, member * out_width, out_width, 1)
    mixed = jnp.dot(
        lax.all_gather(aggregate, "feat", axis=1, tiled=True),
        own_cols,
        preferred_element_type=jnp.float32,
    )
    return jnp.maximum(mixed + bias[None, :], 0.0).astype(jnp.bfloat16)


def solution(mesh):
    in_specs = (
        P("blk", "feat"),
        P("blk", None, None),
        P("blk"),
        P("blk"),
        P("blk"),
        P(),
        P("feat"),
    )
    out_specs = P("blk", "feat")
    return jax.shard_map(body, mesh=mesh, in_specs=in_specs, out_specs=out_specs, check_vma=False)
```

profile of v0, /device:TPU:0, one launch (start us, length us, event | category | flops | bytes accessed | tf_op | source)
XLA Modules:
  0.0 183.8 jit_solution(13651544771678281297)
XLA Ops:
  6.5 0.0 all-gather.2.cloned.1.call-start
  6.5 0.5 collective-permute-start
  7.0 1.0 compare_and_fusion
  8.0 1.6 fusion.107
  9.7 1.8 gather_fusion
  11.5 0.6 iota_compare_fusion.9
  12.1 0.7 iota_compare_fusion.10
  12.8 0.7 iota_compare_fusion.11
  13.5 0.7 iota_compare_fusion.12
  14.2 0.6 iota_compare_fusion.13
  14.7 0.6 iota_compare_fusion.14
  15.4 4.4 %collective-permute-done = bf16[3072,128]{1,0:T(8,128)(2,1)S(1)} collective-permute-done((bf16[3072,128]{1,0:T(8,128)(2,1)}, bf16[3072,128]{1,0:T(8,128)(2,1)S(1)}, u32[]{:S(2)}, u32[]{:S(2)}) %collective-permute-start) | collective-permute-done | bytes 786464 | tf_op jit(solution)/shard_map/ppermute | solution.py:9
  19.8 0.0 collective-permute-start.1
  19.8 0.5 iota_compare_fusion.15
  20.4 1.7 fusion.31
  22.1 10.1 %collective-permute-done.1 = bf16[3072,128]{1,0:T(8,128)(2,1)} collective-permute-done((bf16[3072,128]{1,0:T(8,128)(2,1)S(1)}, bf16[3072,128]{1,0:T(8,128)(2,1)}, u32[]{:S(2)}, u32[]{:S(2)}) %collective-permute-start.1) | collective-permute-done | bytes 786464 | tf_op jit(solution)/shard_map/ppermute | solution.py:9
  32.2 0.0 collective-permute-start.2
  32.2 0.0 copy-done.1
  32.2 0.6 iota_compare_fusion.8
  32.8 0.5 copy.9
  33.4 0.1 fusion.108
  33.5 0.9 fusion.15
  34.4 1.8 gather_fusion.1
  36.2 8.7 %collective-permute-done.2 = bf16[3072,128]{1,0:T(8,128)(2,1)} collective-permute-done((bf16[3072,128]{1,0:T(8,128)(2,1)}, bf16[3072,128]{1,0:T(8,128)(2,1)}, u32[]{:S(2)}, u32[]{:S(2)}) %collective-permute-start.2) | collective-permute-done | bytes 786464 | tf_op jit(solution)/shard_map/ppermute | solution.py:9
  44.8 0.0 collective-permute-start.3
  44.8 2.7 %fusion.29 = f32[16,128,128]{2,1,0:T(8,128)} fusion(bf16[16,128,128]{2,1,0:T(8,128)(2,1)S(1)} %gather_fusion.1, bf16[128,128,128]{2,1,0:T(8,128)(2,1)} %param.10, pred[16]{0:T(512)(128)(4,1)S(1)} %get-tuple-element.46), kind=kOutput, calls=%fused_computation.39 | convolution fusion | flops 67371008 | bytes 2097168 | tf_op jit(solution)/shard_map/ktj,kjf->ktf/dot_general | solution.py:20
  47.5 1.7 copy.10
  49.2 2.1 %fusion.13 = f32[24,128,128]{2,0,1:T(8,128)} fusion(f32[16,128,128]{1,0,2:T(8,128)S(1)} %copy.10, s32[16]{0:T(128)S(1)} %get-tuple-element.35, pred[16]{0:T(512)(128)(4,1)S(1)} %iota_compare_fusion.14), kind=kOutput, calls=%fused_computation.23 | convolution fusion | flops 75498240 | bytes 2621520 | tf_op jit(solution)/shard_map/rk,ktf->rtf/dot_general | solution.py:27
  51.3 1.8 gather_fusion.2
  53.1 2.7 %fusion.27 = f32[16,128,128]{2,1,0:T(8,128)} fusion(bf16[16,128,128]{2,1,0:T(8,128)(2,1)S(1)} %gather_fusion.2, bf16[128,128,128]{2,1,0:T(8,128)(2,1)} %param.10, pred[16]{0:T(512)(128)(4,1)S(1)} %get-tuple-element.44), kind=kOutput, calls=%fused_computation.37 | convolution fusion | flops 67371008 | bytes 2097168 | tf_op jit(solution)/shard_map/ktj,kjf->ktf/dot_general | solution.py:20
  55.8 1.7 copy.11
  57.6 0.0 collective-permute-done.3
  57.6 0.1 collective-permute-start.4
  57.6 2.0 %fusion.11 = f32[24,128,128]{2,0,1:T(8,128)} fusion(f32[16,128,128]{1,0,2:T(8,128)S(1)} %copy.11, s32[16]{0:T(128)S(1)} %get-tuple-element.34, pred[16]{0:T(512)(128)(4,1)S(1)} %iota_compare_fusion.13), kind=kOutput, calls=%fused_computation.21 | convolution fusion | flops 75498240 | bytes 2621520 | tf_op jit(solution)/shard_map/rk,ktf->rtf/dot_general | solution.py:27
  59.7 1.8 gather_fusion.3
  61.5 2.7 %fusion.25 = f32[16,128,128]{2,1,0:T(8,128)} fusion(bf16[16,128,128]{2,1,0:T(8,128)(2,1)S(1)} %gather_fusion.3, bf16[128,128,128]{2,1,0:T(8,128)(2,1)} %param.10, pred[16]{0:T(512)(128)(4,1)S(1)} %get-tuple-element.42), kind=kOutput, calls=%fused_computation.35 | convolution fusion | flops 67371008 | bytes 2097168 | tf_op jit(solution)/shard_map/ktj,kjf->ktf/dot_general | solution.py:20
  64.2 1.7 copy.12
  66.0 2.1 %fusion.9 = f32[24,128,128]{2,0,1:T(8,128)} fusion(f32[16,128,128]{1,0,2:T(8,128)S(1)} %copy.12, s32[16]{0:T(128)S(1)} %get-tuple-element.33, pred[16]{0:T(512)(128)(4,1)S(1)} %iota_compare_fusion.12), kind=kOutput, calls=%fused_computation.19 | convolution fusion | flops 75498240 | bytes 2621520 | tf_op jit(solution)/shard_map/rk,ktf->rtf/dot_general | solution.py:27
  68.0 1.8 gather_fusion.4
  69.8 0.5 collective-permute-done.4
  70.3 0.2 collective-permute-start.5
  70.4 2.7 %fusion.23 = f32[16,128,128]{2,1,0:T(8,128)} fusion(bf16[16,128,128]{2,1,0:T(8,128)(2,1)S(1)} %gather_fusion.4, bf16[128,128,128]{2,1,0:T(8,128)(2,1)} %param.10, pred[16]{0:T(512)(128)(4,1)S(1)} %get-tuple-element.40), kind=kOutput, calls=%fused_computation.33 | convolution fusion | flops 67371008 | bytes 2097168 | tf_op jit(solution)/shard_map/ktj,kjf->ktf/dot_general | solution.py:20
  73.1 1.7 copy.13
  74.9 2.1 %fusion.7 = f32[24,128,128]{2,0,1:T(8,128)} fusion(f32[16,128,128]{1,0,2:T(8,128)S(1)} %copy.13, s32[16]{0:T(128)S(1)} %get-tuple-element.32, pred[16]{0:T(512)(128)(4,1)S(1)} %iota_compare_fusion.11), kind=kOutput, calls=%fused_computation.17 | convolution fusion | flops 75498240 | bytes 2621520 | tf_op jit(solution)/shard_map/rk,ktf->rtf/dot_general | solution.py:27
  77.0 1.8 gather_fusion.5
  78.8 2.7 %fusion.21 = f32[16,128,128]{2,1,0:T(8,128)} fusion(bf16[16,128,128]{2,1,0:T(8,128)(2,1)S(1)} %gather_fusion.5, bf16[128,128,128]{2,1,0:T(8,128)(2,1)} %param.10, pred[16]{0:T(512)(128)(4,1)S(1)} %get-tuple-element.38), kind=kOutput, calls=%fused_computation.31 | convolution fusion | flops 67371008 | bytes 2097168 | tf_op jit(solution)/shard_map/ktj,kjf->ktf/dot_general | solution.py:20
  81.5 1.7 copy.14
  83.2 0.0 collective-permute-done.5
  83.2 3.6 %collective-permute-start.6 = (bf16[3072,128]{1,0:T(8,128)(2,1)}, bf16[3072,128]{1,0:T(8,128)(2,1)}, u32[]{:S(2)}, u32[]{:S(2)}) collective-permute-start(bf16[3072,128]{1,0:T(8,128)(2,1)} %collective-permute-done.5), channel_id=1, source_target_pairs={{0,4},{4,8},{8,12},{12,16},{16,20},{20,24},{24,28},{28,0},{1,5},{5... | collective-permute-start | bytes 2359304 | tf_op jit(solution)/shard_map/ppermute | solution.py:9
  86.8 2.0 %fusion.5 = f32[24,128,128]{2,0,1:T(8,128)} fusion(f32[16,128,128]{1,0,2:T(8,128)S(1)} %copy.14, s32[16]{0:T(128)S(1)} %get-tuple-element.31, pred[16]{0:T(512)(128)(4,1)S(1)} %iota_compare_fusion.10), kind=kOutput, calls=%fused_computation.15 | convolution fusion | flops 75498240 | bytes 2621520 | tf_op jit(solution)/shard_map/rk,ktf->rtf/dot_general | solution.py:27
  88.9 1.8 gather_fusion.6
  90.7 2.8 %fusion.19 = f32[16,128,128]{2,1,0:T(8,128)} fusion(bf16[16,128,128]{2,1,0:T(8,128)(2,1)S(1)} %gather_fusion.6, bf16[128,128,128]{2,1,0:T(8,128)(2,1)} %param.10, pred[16]{0:T(512)(128)(4,1)S(1)} %get-tuple-element.50), kind=kOutput, calls=%fused_computation.29 | convolution fusion | flops 67371008 | bytes 2097168 | tf_op jit(solution)/shard_map/ktj,kjf->ktf/dot_general | solution.py:20
  93.4 1.7 copy.15
  95.2 2.1 %fusion.3 = f32[24,128,128]{2,0,1:T(8,128)} fusion(f32[16,128,128]{1,0,2:T(8,128)S(1)} %copy.15, s32[16]{0:T(128)S(1)} %get-tuple-element.37, pred[16]{0:T(512)(128)(4,1)S(1)} %iota_compare_fusion.9), kind=kOutput, calls=%fused_computation.13 | convolution fusion | flops 75498240 | bytes 2621520 | tf_op jit(solution)/shard_map/rk,ktf->rtf/dot_general | solution.py:27
  97.3 0.0 collective-permute-done.6
  97.3 1.8 gather_fusion.7
  99.1 2.7 %fusion.17 = f32[16,128,128]{2,1,0:T(8,128)} fusion(bf16[16,128,128]{2,1,0:T(8,128)(2,1)S(1)} %gather_fusion.7, bf16[128,128,128]{2,1,0:T(8,128)(2,1)} %param.10, pred[16]{0:T(512)(128)(4,1)S(1)} %get-tuple-element.6), kind=kOutput, calls=%fused_computation.27 | convolution fusion | flops 67371008 | bytes 2097168 | tf_op jit(solution)/shard_map/ktj,kjf->ktf/dot_general | solution.py:20
  101.8 1.7 copy.16
  103.5 5.0 %add_convert_fusion = bf16[24,128,128]{2,0,1:T(8,128)(2,1)S(1)} fusion(f32[24,128,128]{2,0,1:T(8,128)} %fusion.3, f32[24,128,128]{2,0,1:T(8,128)} %fusion.5, f32[24,128,128]{2,0,1:T(8,128)} %fusion.7, f32[24,128,128]{2,0,1:T(8,128)} %fusion.9, f32[24,128,128]{2,0,1:T(8,128)} %fusion.11, f32[24,128,128]{2,0,1:T(8,128)S(1)} %fusion.15, ...), kind=kOutput, calls=%fused_computation.11 | convolution fusion | flops 78643968 | bytes 12845136 | tf_op jit(solution)/shard_map/rk,ktf->rtf/dot_general | solution.py:27
  108.6 0.0 copy-start.3
  108.6 1.1 copy.8
  109.6 0.0 all-gather.2.cloned.1.call-update
  109.7 63.5 %all-gather.2.cloned.1.call-done = bf16[3072,512]{1,0:T(8,128)(2,1)} async-done(((bf16[3072,128]{1,0:T(8,128)(2,1)}), bf16[3072,512]{1,0:T(8,128)(2,1)}) %all-gather.2.cloned.1.call-update) | async-done | bytes 3145744 | tf_op jit(solution)/shard_map/all_gather | solution.py:52
  173.2 3.8 %fusion.1 = bf16[3072,128]{1,0:T(8,128)(2,1)} fusion(bf16[3072,512]{1,0:T(8,128)(2,1)} %all-gather.2.cloned.1.call-done, f32[128]{0:T(128)S(1)} %copy-done.3, bf16[512,512]{1,0:T(8,128)(2,1)S(1)} %copy-done, s32[]{:T(128)S(6)} %select_n.10), kind=kOutput, calls=%fused_computation.10 | convolution fusion | flops 403832832 | bytes 4063748 | tf_op jit(solution)/shard_map/dot_general | solution.py:51
  (14 shorter events, 0.1 us)
Async XLA Ops:
  6.5 166.7 %copy-start = (bf16[512,512]{1,0:T(8,128)(2,1)S(1)}, bf16[512,512]{1,0:T(8,128)(2,1)}, u32[]{:S(2)}) copy-start(bf16[512,512]{1,0:T(8,128)(2,1)} %param.14) | copy-start | bytes 1572868
  6.5 166.7 %all-gather.2.cloned.1.call-start = ((), (), s32[]{:S(2)}) async-start(), calls=%async_computation | async-start | bytes 3932160 | tf_op jit(solution)/shard_map/all_gather | solution.py:52
  6.5 13.2 %collective-permute-start = (bf16[3072,128]{1,0:T(8,128)(2,1)}, bf16[3072,128]{1,0:T(8,128)(2,1)S(1)}, u32[]{:S(2)}, u32[]{:S(2)}) collective-permute-start(bf16[3072,128]{1,0:T(8,128)(2,1)} %param.9), channel_id=1, source_target_pairs={{0,4},{4,8},{8,12},{12,16},{16,20},{20,24},{24,28},{28,0},{1,5},{5... | collective-permute-start | bytes 2359304 | tf_op jit(solution)/shard_map/ppermute | solution.py:9
  19.8 12.4 %copy-start.1 = (bf16[3072,128]{1,0:T(8,128)(2,1)}, bf16[3072,128]{1,0:T(8,128)(2,1)S(1)}, u32[]{:S(2)}) copy-start(bf16[3072,128]{1,0:T(8,128)(2,1)S(1)} %collective-permute-done) | copy-start | bytes 2359300
  19.8 12.4 %collective-permute-start.1 = (bf16[3072,128]{1,0:T(8,128)(2,1)S(1)}, bf16[3072,128]{1,0:T(8,128)(2,1)}, u32[]{:S(2)}, u32[]{:S(2)}) collective-permute-start(bf16[3072,128]{1,0:T(8,128)(2,1)S(1)} %collective-permute-done), channel_id=1, source_target_pairs={{0,4},{4,8},{8,12},{12,16},{16,20},{20,24},{24,28},{28,0},{1,5},{5... | collective-permute-start | bytes 2359304 | tf_op jit(solution)/shard_map/ppermute | solution.py:9
  22.1 11.3 %copy-start.2 = (s32[128]{0:T(128)S(1)}, s32[128]{0:T(128)}, u32[]{:S(2)}) copy-start(s32[128]{0:T(128)} %param.11) | copy-start | bytes 1540
  32.2 12.6 %collective-permute-start.2 = (bf16[3072,128]{1,0:T(8,128)(2,1)}, bf16[3072,128]{1,0:T(8,128)(2,1)}, u32[]{:S(2)}, u32[]{:S(2)}) collective-permute-start(bf16[3072,128]{1,0:T(8,128)(2,1)} %collective-permute-done.1), channel_id=1, source_target_pairs={{0,4},{4,8},{8,12},{12,16},{16,20},{20,24},{24,28},{28,0},{1,5},{5... | collective-permute-start | bytes 2359304 | tf_op jit(solution)/shard_map/ppermute | solution.py:9
  44.8 12.8 %collective-permute-start.3 = (bf16[3072,128]{1,0:T(8,128)(2,1)}, bf16[3072,128]{1,0:T(8,128)(2,1)}, u32[]{:S(2)}, u32[]{:S(2)}) collective-permute-start(bf16[3072,128]{1,0:T(8,128)(2,1)} %collective-permute-done.2), channel_id=1, source_target_pairs={{0,4},{4,8},{8,12},{12,16},{16,20},{20,24},{24,28},{28,0},{1,5},{5... | collective-permute-start | bytes 2359304 | tf_op jit(solution)/shard_map/ppermute | solution.py:9
  57.6 12.7 %collective-permute-start.4 = (bf16[3072,128]{1,0:T(8,128)(2,1)}, bf16[3072,128]{1,0:T(8,128)(2,1)}, u32[]{:S(2)}, u32[]{:S(2)}) collective-permute-start(bf16[3072,128]{1,0:T(8,128)(2,1)} %collective-permute-done.3), channel_id=1, source_target_pairs={{0,4},{4,8},{8,12},{12,16},{16,20},{20,24},{24,28},{28,0},{1,5},{5... | collective-permute-start | bytes 2359304 | tf_op jit(solution)/shard_map/ppermute | solution.py:9
  70.3 13.0 %collective-permute-start.5 = (bf16[3072,128]{1,0:T(8,128)(2,1)}, bf16[3072,128]{1,0:T(8,128)(2,1)}, u32[]{:S(2)}, u32[]{:S(2)}) collective-permute-start(bf16[3072,128]{1,0:T(8,128)(2,1)} %collective-permute-done.4), channel_id=1, source_target_pairs={{0,4},{4,8},{8,12},{12,16},{16,20},{20,24},{24,28},{28,0},{1,5},{5... | collective-permute-start | bytes 2359304 | tf_op jit(solution)/shard_map/ppermute | solution.py:9
  83.2 14.1 %collective-permute-start.6 = (bf16[3072,128]{1,0:T(8,128)(2,1)}, bf16[3072,128]{1,0:T(8,128)(2,1)}, u32[]{:S(2)}, u32[]{:S(2)}) collective-permute-start(bf16[3072,128]{1,0:T(8,128)(2,1)} %collective-permute-done.5), channel_id=1, source_target_pairs={{0,4},{4,8},{8,12},{12,16},{16,20},{20,24},{24,28},{28,0},{1,5},{5... | collective-permute-start | bytes 2359304 | tf_op jit(solution)/shard_map/ppermute | solution.py:9
  108.6 64.7 %copy-start.3 = (f32[128]{0:T(128)S(1)}, f32[128]{0:T(128)}, u32[]{:S(2)}) copy-start(f32[128]{0:T(128)} %param.15) | copy-start | bytes 1540
Sparse Core Ops, SparseCore 0:
  109.8 63.3 all-gather.1
where the time goes:
time: 185 us; the launch traced here: 184 us
  waiting for transfers between devices  87.2 us (47%)
  matrix products  42.9 us (23%)
  local copies, waits for them, and re-layouts  29.6 us (16%)
  between operations  13.7 us (7%)
  other arithmetic  6.13 us (3%)
  starting transfers between devices  4.29 us (2%)
    all_gather x1, waiting for transfers between devices, body(): lax.all_gather(aggregate, 'feat', axis=1, tiled=True)  63.5 us
    ppermute x7, waiting for transfers between devices, shifted(): lax.ppermute(shard, axis, [(i, (i + by) % count) for i in range(count)])  23.6 us
    dot_general x8, matrix products, add_tiles(): jnp.einsum('ktj,kjf->ktf', values_all[offset], picked, preferred_element_...  20.8 us
    dot_general x8, matrix products, add_tiles(): jnp.einsum('rk,ktf->rtf', one_hot, products, precision=lax.Precision.HIGH...  18.4 us
    gather x8, local copies, waits for them, and re-layouts, pick_tiles(): return jnp.take(source, wanted, axis=0)  14.2 us
    dot_general x8, local copies, waits for them, and re-layouts, add_tiles(): jnp.einsum('ktj,kjf->ktf', values_all[offset], picked, preferred_element_...  12.6 us
    lt x8, other arithmetic, add_tiles(): active = jnp.arange(slot_count) < tile_counts[offset]  5.05 us
    ppermute x7, starting transfers between devices, shifted(): lax.ppermute(shard, axis, [(i, (i + by) % count) for i in range(count)])  4.28 us
  transfers between devices with their start and end apart: 8, of which 5 were waited for; matrix products, arithmetic and copies ran while one was open for 34% of the time, Pallas kernels for 0%

commit v1 on v0

--- a/solution.py
+++ b/solution.py
@@ -1,7 +1,27 @@
+import functools
 import jax
 import jax.numpy as jnp
 from jax import lax
 from jax.sharding import PartitionSpec as P
+
+
+def drive_the_works(raw, mesh_name, in_dim):
+    devs = lax.axis_size(mesh_name)
+    crops = [(p, (p + 1) % devs) for p in range(devs)]
+    sides = [(p, (p - 1) % devs) for p in range(devs)]
+    r_now, t_next = ([raw], [raw])
+    for _ in range(devs // 2):
+        carry_in = lax.ppermute(r_now[-1], mesh_name, crops)
+        r_now.append(carry_in)
+    for _ in tuple(range((devs - 1) // 2)):
+        m_next = lax.ppermute(t_next[-1], mesh_name, sides)
+        t_next.append(m_next)
+    big = jnp.concatenate([*r_now[::-1], *t_next[1:]], axis=in_dim)
+    u_next = lax.axis_index(mesh_name)
+    return jnp.roll(big, shift=(u_next - devs // 2) * raw.shape[in_dim], axis=in_dim)
+
+
+advance_spots = functools.partial(drive_the_works, mesh_name="feat", in_dim=1)
 
 
 def shifted(shard, axis, by):
@@ -48,11 +68,7 @@
     out_width = bias.shape[0]
     member = lax.axis_index("feat")
     own_cols = lax.dynamic_slice_in_dim(weight, member * out_width, out_width, 1)
-    mixed = jnp.dot(
-        lax.all_gather(aggregate, "feat", axis=1, tiled=True),
-        own_cols,
-        preferred_element_type=jnp.float32,
-    )
+    mixed = jnp.dot(advance_spots(aggregate), own_cols, preferred_element_type=jnp.float32)
     return jnp.maximum(mixed + bias[None, :], 0.0).astype(jnp.bfloat16)
 
 

time: 185 us -> 164 us (0.89)
  between operations: 13.7 us -> 0.41 us
  waiting for transfers between devices: 87.2 us -> 74.3 us
  starting transfers between devices: 4.29 us -> 9.74 us
  matrix products: 42.9 us -> 41 us
    all_gather x1 -> x0, waiting for transfers between devices: 63.5 us -> none  [body(): lax.all_gather(aggregate, 'feat', axis=1, tiled=True)]
    ppermute x0 -> x3, waiting for transfers between devices: none -> 50.7 us  [the longest x2 38.2 us: drive_the_works(): carry_in = lax.ppermute(r_now[-1], mesh_name, crops)]
    ppermute x0 -> x3, starting transfers between devices: none -> 5.45 us  [the longest x1 3.82 us: drive_the_works(): m_next = lax.ppermute(t_next[-1], mesh_name, sides)]
    dot_general x1, matrix products: 3.76 us -> 1.87 us  [body(): jnp.dot(advance_spots(aggregate), own_cols, preferred_element_type=jnp.fl...]
  transfers between devices with their start and end apart: 8 -> 10, of which waited for: 5 -> 7; matrix products, arithmetic and copies ran while one was open for 34% -> 39% of each run, Pallas kernels for 0% -> 0%
where the time goes in v1:
time: 164 us; the launch traced here: 162 us
  waiting for transfers between devices  74.3 us (45%)
  matrix products  41 us (25%)
  local copies, waits for them, and re-layouts  30.8 us (19%)
  starting transfers between devices  9.74 us (6%)
  other arithmetic  6.13 us (4%)
    ppermute x2, waiting for transfers between devices, drive_the_works(): carry_in = lax.ppermute(r_now[-1], mesh_name, crops)  38.2 us
    ppermute x7, waiting for transfers between devices, shifted(): lax.ppermute(shard, axis, [(i, (i + by) % count) for i in range(count)])  23.6 us
    dot_general x8, matrix products, add_tiles(): jnp.einsum('ktj,kjf->ktf', values_all[offset], picked, preferred_element_...  20.8 us
    dot_general x8, matrix products, add_tiles(): jnp.einsum('rk,ktf->rtf', one_hot, products, precision=lax.Precision.HIGH...  18.4 us
    gather x8, local copies, waits for them, and re-layouts, pick_tiles(): return jnp.take(source, wanted, axis=0)  14.2 us
    dot_general x8, local copies, waits for them, and re-layouts, add_tiles(): jnp.einsum('ktj,kjf->ktf', values_all[offset], picked, preferred_element_...  12.6 us
    ppermute x1, waiting for transfers between devices, drive_the_works(): m_next = lax.ppermute(t_next[-1], mesh_name, sides)  12.5 us
    lt x8, other arithmetic, add_tiles(): active = jnp.arange(slot_count) < tile_counts[offset]  5.05 us
  transfers between devices with their start and end apart: 10, of which 7 were waited for; matrix products, arithmetic and copies ran while one was open for 39% of the time, Pallas kernels for 0%

profile of v1, /device:TPU:0, one launch (start us, length us, event | category | flops | bytes accessed | tf_op | source)
XLA Modules:
  0.0 162.4 jit_solution(13270635384834760461)
XLA Ops:
  0.0 0.5 collective-permute-start
  0.5 1.0 compare_and_fusion
  1.5 1.6 %fusion.108 = (s32[1]{0:T(128)}, s32[1]{0:T(128)}, s32[1]{0:T(128)}, s32[1]{0:T(128)}, s32[1]{0:T(128)}, /*index=5*/s32[1]{0:T(128)}, s32[1]{0:T(128)}, s32[1]{0:T(128)}) fusion(s32[8]{0:T(128)} %param.13), kind=kLoop, calls=%fused_computation.158 | loop fusion | bytes 64 | tf_op jit(solution)/shard_map/slice | solution.py:43
  3.1 1.8 %gather_fusion = bf16[16,128,128]{2,1,0:T(8,128)(2,1)S(1)} fusion(bf16[24,128,128]{2,1,0:T(8,128)(2,1)} %bitcast.69, s32[1024]{0:T(1024)S(1)} %pad_clamp_fusion.7), kind=kCustom, calls=%fused_computation.clone | custom fusion | bytes 1048640 | tf_op jit(solution)/shard_map/jit(_take)/gather | solution.py:34
  4.9 0.6 iota_compare_fusion.9
  5.6 0.7 iota_compare_fusion.10
  6.2 0.7 iota_compare_fusion.11
  6.9 0.7 iota_compare_fusion.12
  7.6 0.6 iota_compare_fusion.13
  8.2 0.6 iota_compare_fusion.14
  8.8 4.4 %collective-permute-done = bf16[3072,128]{1,0:T(8,128)(2,1)S(1)} collective-permute-done((bf16[3072,128]{1,0:T(8,128)(2,1)}, bf16[3072,128]{1,0:T(8,128)(2,1)S(1)}, u32[]{:S(2)}, u32[]{:S(2)}) %collective-permute-start) | collective-permute-done | bytes 786464 | tf_op jit(solution)/shard_map/ppermute | solution.py:29
  13.2 0.5 iota_compare_fusion.15
  13.8 1.7 %fusion.32 = f32[16,128,128]{2,1,0:T(8,128)S(1)} fusion(bf16[16,128,128]{2,1,0:T(8,128)(2,1)S(1)} %gather_fusion, bf16[128,128,128]{2,1,0:T(8,128)(2,1)} %param.10, pred[16]{0:T(512)(128)(4,1)S(1)} %get-tuple-element.48), kind=kOutput, calls=%fused_computation.42 | convolution fusion | flops 67371008 | bytes 2097168 | tf_op jit(solution)/shard_map/ktj,kjf->ktf/dot_general | solution.py:40
  15.6 10.1 %collective-permute-done.1 = bf16[3072,128]{1,0:T(8,128)(2,1)} collective-permute-done((bf16[3072,128]{1,0:T(8,128)(2,1)S(1)}, bf16[3072,128]{1,0:T(8,128)(2,1)}, u32[]{:S(2)}, u32[]{:S(2)}) %collective-permute-start.1) | collective-permute-done | bytes 786464 | tf_op jit(solution)/shard_map/ppermute | solution.py:29
  25.7 0.6 iota_compare_fusion.8
  26.3 0.5 copy.9
  26.9 0.9 fusion.16
  27.8 1.8 %gather_fusion.1 = bf16[16,128,128]{2,1,0:T(8,128)(2,1)S(1)} fusion(bf16[24,128,128]{2,1,0:T(8,128)(2,1)} %bitcast.70, s32[1024]{0:T(1024)S(1)} %pad_clamp_fusion.6), kind=kCustom, calls=%fused_computation.1.clone | custom fusion | bytes 1048640 | tf_op jit(solution)/shard_map/jit(_take)/gather | solution.py:34
  29.6 8.7 %collective-permute-done.2 = bf16[3072,128]{1,0:T(8,128)(2,1)} collective-permute-done((bf16[3072,128]{1,0:T(8,128)(2,1)}, bf16[3072,128]{1,0:T(8,128)(2,1)}, u32[]{:S(2)}, u32[]{:S(2)}) %collective-permute-start.2) | collective-permute-done | bytes 786464 | tf_op jit(solution)/shard_map/ppermute | solution.py:29
  38.3 2.7 %fusion.30 = f32[16,128,128]{2,1,0:T(8,128)} fusion(bf16[16,128,128]{2,1,0:T(8,128)(2,1)S(1)} %gather_fusion.1, bf16[128,128,128]{2,1,0:T(8,128)(2,1)} %param.10, pred[16]{0:T(512)(128)(4,1)S(1)} %get-tuple-element.46), kind=kOutput, calls=%fused_computation.40 | convolution fusion | flops 67371008 | bytes 2097168 | tf_op jit(solution)/shard_map/ktj,kjf->ktf/dot_general | solution.py:40
  41.0 1.7 %copy.10 = f32[16,128,128]{1,0,2:T(8,128)S(1)} copy(f32[16,128,128]{2,1,0:T(8,128)} %fusion.30) | data formatting | bytes 2097152 | tf_op jit(solution)/shard_map/ktj,kjf->ktf/dot_general | solution.py:40
  42.7 2.1 %fusion.14 = f32[24,128,128]{2,0,1:T(8,128)} fusion(f32[16,128,128]{1,0,2:T(8,128)S(1)} %copy.10, s32[16]{0:T(128)S(1)} %get-tuple-element.35, pred[16]{0:T(512)(128)(4,1)S(1)} %iota_compare_fusion.14), kind=kOutput, calls=%fused_computation.24 | convolution fusion | flops 75498240 | bytes 2621520 | tf_op jit(solution)/shard_map/rk,ktf->rtf/dot_general | solution.py:47
  44.8 1.8 %gather_fusion.2 = bf16[16,128,128]{2,1,0:T(8,128)(2,1)S(1)} fusion(bf16[24,128,128]{2,1,0:T(8,128)(2,1)} %bitcast.10, s32[1024]{0:T(1024)S(1)} %pad_clamp_fusion.5), kind=kCustom, calls=%fused_computation.2.clone | custom fusion | bytes 1048640 | tf_op jit(solution)/shard_map/jit(_take)/gather | solution.py:34
  46.6 2.7 %fusion.28 = f32[16,128,128]{2,1,0:T(8,128)} fusion(bf16[16,128,128]{2,1,0:T(8,128)(2,1)S(1)} %gather_fusion.2, bf16[128,128,128]{2,1,0:T(8,128)(2,1)} %param.10, pred[16]{0:T(512)(128)(4,1)S(1)} %get-tuple-element.44), kind=kOutput, calls=%fused_computation.38 | convolution fusion | flops 67371008 | bytes 2097168 | tf_op jit(solution)/shard_map/ktj,kjf->ktf/dot_general | solution.py:40
  49.3 1.7 %copy.11 = f32[16,128,128]{1,0,2:T(8,128)S(1)} copy(f32[16,128,128]{2,1,0:T(8,128)} %fusion.28) | data formatting | bytes 2097152 | tf_op jit(solution)/shard_map/ktj,kjf->ktf/dot_general | solution.py:40
  51.1 2.0 %fusion.12 = f32[24,128,128]{2,0,1:T(8,128)} fusion(f32[16,128,128]{1,0,2:T(8,128)S(1)} %copy.11, s32[16]{0:T(128)S(1)} %get-tuple-element.34, pred[16]{0:T(512)(128)(4,1)S(1)} %iota_compare_fusion.13), kind=kOutput, calls=%fused_computation.22 | convolution fusion | flops 75498240 | bytes 2621520 | tf_op jit(solution)/shard_map/rk,ktf->rtf/dot_general | solution.py:47
  53.2 1.8 %gather_fusion.3 = bf16[16,128,128]{2,1,0:T(8,128)(2,1)S(1)} fusion(bf16[24,128,128]{2,1,0:T(8,128)(2,1)} %bitcast.14, s32[1024]{0:T(1024)S(1)} %pad_clamp_fusion.4), kind=kCustom, calls=%fused_computation.3.clone | custom fusion | bytes 1048640 | tf_op jit(solution)/shard_map/jit(_take)/gather | solution.py:34
  54.9 2.7 %fusion.26 = f32[16,128,128]{2,1,0:T(8,128)} fusion(bf16[16,128,128]{2,1,0:T(8,128)(2,1)S(1)} %gather_fusion.3, bf16[128,128,128]{2,1,0:T(8,128)(2,1)} %param.10, pred[16]{0:T(512)(128)(4,1)S(1)} %get-tuple-element.42), kind=kOutput, calls=%fused_computation.36 | convolution fusion | flops 67371008 | bytes 2097168 | tf_op jit(solution)/shard_map/ktj,kjf->ktf/dot_general | solution.py:40
  57.7 1.7 %copy.12 = f32[16,128,128]{1,0,2:T(8,128)S(1)} copy(f32[16,128,128]{2,1,0:T(8,128)} %fusion.26) | data formatting | bytes 2097152 | tf_op jit(solution)/shard_map/ktj,kjf->ktf/dot_general | solution.py:40
  59.4 2.1 %fusion.10 = f32[24,128,128]{2,0,1:T(8,128)} fusion(f32[16,128,128]{1,0,2:T(8,128)S(1)} %copy.12, s32[16]{0:T(128)S(1)} %get-tuple-element.33, pred[16]{0:T(512)(128)(4,1)S(1)} %iota_compare_fusion.12), kind=kOutput, calls=%fused_computation.20 | convolution fusion | flops 75498240 | bytes 2621520 | tf_op jit(solution)/shard_map/rk,ktf->rtf/dot_general | solution.py:47
  61.5 1.8 %gather_fusion.4 = bf16[16,128,128]{2,1,0:T(8,128)(2,1)S(1)} fusion(bf16[24,128,128]{2,1,0:T(8,128)(2,1)} %bitcast.18, s32[1024]{0:T(1024)S(1)} %pad_clamp_fusion.3), kind=kCustom, calls=%fused_computation.4.clone | custom fusion | bytes 1048640 | tf_op jit(solution)/shard_map/jit(_take)/gather | solution.py:34
  63.3 0.5 collective-permute-done.4
  63.7 0.2 collective-permute-start.5
  63.9 2.7 %fusion.24 = f32[16,128,128]{2,1,0:T(8,128)} fusion(bf16[16,128,128]{2,1,0:T(8,128)(2,1)S(1)} %gather_fusion.4, bf16[128,128,128]{2,1,0:T(8,128)(2,1)} %param.10, pred[16]{0:T(512)(128)(4,1)S(1)} %get-tuple-element.40), kind=kOutput, calls=%fused_computation.34 | convolution fusion | flops 67371008 | bytes 2097168 | tf_op jit(solution)/shard_map/ktj,kjf->ktf/dot_general | solution.py:40
  66.6 1.7 %copy.13 = f32[16,128,128]{1,0,2:T(8,128)S(1)} copy(f32[16,128,128]{2,1,0:T(8,128)} %fusion.24) | data formatting | bytes 2097152 | tf_op jit(solution)/shard_map/ktj,kjf->ktf/dot_general | solution.py:40
  68.3 2.1 %fusion.8 = f32[24,128,128]{2,0,1:T(8,128)} fusion(f32[16,128,128]{1,0,2:T(8,128)S(1)} %copy.13, s32[16]{0:T(128)S(1)} %get-tuple-element.32, pred[16]{0:T(512)(128)(4,1)S(1)} %iota_compare_fusion.11), kind=kOutput, calls=%fused_computation.18 | convolution fusion | flops 75498240 | bytes 2621520 | tf_op jit(solution)/shard_map/rk,ktf->rtf/dot_general | solution.py:47
  70.4 1.8 %gather_fusion.5 = bf16[16,128,128]{2,1,0:T(8,128)(2,1)S(1)} fusion(bf16[24,128,128]{2,1,0:T(8,128)(2,1)} %bitcast.22, s32[1024]{0:T(1024)S(1)} %pad_clamp_fusion.2), kind=kCustom, calls=%fused_computation.5.clone | custom fusion | bytes 1048640 | tf_op jit(solution)/shard_map/jit(_take)/gather | solution.py:34
  72.2 2.7 %fusion.22 = f32[16,128,128]{2,1,0:T(8,128)} fusion(bf16[16,128,128]{2,1,0:T(8,128)(2,1)S(1)} %gather_fusion.5, bf16[128,128,128]{2,1,0:T(8,128)(2,1)} %param.10, pred[16]{0:T(512)(128)(4,1)S(1)} %get-tuple-element.38), kind=kOutput, calls=%fused_computation.32 | convolution fusion | flops 67371008 | bytes 2097168 | tf_op jit(solution)/shard_map/ktj,kjf->ktf/dot_general | solution.py:40
  74.9 1.7 %copy.14 = f32[16,128,128]{1,0,2:T(8,128)S(1)} copy(f32[16,128,128]{2,1,0:T(8,128)} %fusion.22) | data formatting | bytes 2097152 | tf_op jit(solution)/shard_map/ktj,kjf->ktf/dot_general | solution.py:40
  76.7 3.6 %collective-permute-start.6 = (bf16[3072,128]{1,0:T(8,128)(2,1)}, bf16[3072,128]{1,0:T(8,128)(2,1)}, u32[]{:S(2)}, u32[]{:S(2)}) collective-permute-start(bf16[3072,128]{1,0:T(8,128)(2,1)} %collective-permute-done.5), channel_id=1, source_target_pairs={{0,4},{4,8},{8,12},{12,16},{16,20},{20,24},{24,28},{28,0},{1,5},{5... | collective-permute-start | bytes 2359304 | tf_op jit(solution)/shard_map/ppermute | solution.py:29
  80.3 2.0 %fusion.6 = f32[24,128,128]{2,0,1:T(8,128)} fusion(f32[16,128,128]{1,0,2:T(8,128)S(1)} %copy.14, s32[16]{0:T(128)S(1)} %get-tuple-element.31, pred[16]{0:T(512)(128)(4,1)S(1)} %iota_compare_fusion.10), kind=kOutput, calls=%fused_computation.16 | convolution fusion | flops 75498240 | bytes 2621520 | tf_op jit(solution)/shard_map/rk,ktf->rtf/dot_general | solution.py:47
  82.3 1.8 %gather_fusion.6 = bf16[16,128,128]{2,1,0:T(8,128)(2,1)S(1)} fusion(bf16[24,128,128]{2,1,0:T(8,128)(2,1)} %bitcast.26, s32[1024]{0:T(1024)S(1)} %pad_clamp_fusion.1), kind=kCustom, calls=%fused_computation.6.clone | custom fusion | bytes 1048640 | tf_op jit(solution)/shard_map/jit(_take)/gather | solution.py:34
  84.1 2.8 %fusion.20 = f32[16,128,128]{2,1,0:T(8,128)} fusion(bf16[16,128,128]{2,1,0:T(8,128)(2,1)S(1)} %gather_fusion.6, bf16[128,128,128]{2,1,0:T(8,128)(2,1)} %param.10, pred[16]{0:T(512)(128)(4,1)S(1)} %get-tuple-element.50), kind=kOutput, calls=%fused_computation.30 | convolution fusion | flops 67371008 | bytes 2097168 | tf_op jit(solution)/shard_map/ktj,kjf->ktf/dot_general | solution.py:40
  86.9 1.7 %copy.15 = f32[16,128,128]{1,0,2:T(8,128)S(1)} copy(f32[16,128,128]{2,1,0:T(8,128)} %fusion.20) | data formatting | bytes 2097152 | tf_op jit(solution)/shard_map/ktj,kjf->ktf/dot_general | solution.py:40
  88.6 2.1 %fusion.4 = f32[24,128,128]{2,0,1:T(8,128)} fusion(f32[16,128,128]{1,0,2:T(8,128)S(1)} %copy.15, s32[16]{0:T(128)S(1)} %get-tuple-element.37, pred[16]{0:T(512)(128)(4,1)S(1)} %iota_compare_fusion.9), kind=kOutput, calls=%fused_computation.14 | convolution fusion | flops 75498240 | bytes 2621520 | tf_op jit(solution)/shard_map/rk,ktf->rtf/dot_general | solution.py:47
  90.8 1.8 %gather_fusion.7 = bf16[16,128,128]{2,1,0:T(8,128)(2,1)S(1)} fusion(bf16[24,128,128]{2,1,0:T(8,128)(2,1)} %bitcast.30, s32[1024]{0:T(1024)S(1)} %pad_clamp_fusion), kind=kCustom, calls=%fused_computation.7.clone | custom fusion | bytes 1048640 | tf_op jit(solution)/shard_map/jit(_take)/gather | solution.py:34
  92.6 2.7 %fusion.18 = f32[16,128,128]{2,1,0:T(8,128)} fusion(bf16[16,128,128]{2,1,0:T(8,128)(2,1)S(1)} %gather_fusion.7, bf16[128,128,128]{2,1,0:T(8,128)(2,1)} %param.10, pred[16]{0:T(512)(128)(4,1)S(1)} %get-tuple-element.6), kind=kOutput, calls=%fused_computation.28 | convolution fusion | flops 67371008 | bytes 2097168 | tf_op jit(solution)/shard_map/ktj,kjf->ktf/dot_general | solution.py:40
  95.3 1.7 %copy.16 = f32[16,128,128]{1,0,2:T(8,128)S(1)} copy(f32[16,128,128]{2,1,0:T(8,128)} %fusion.18) | data formatting | bytes 2097152 | tf_op jit(solution)/shard_map/ktj,kjf->ktf/dot_general | solution.py:40
  97.0 5.0 %add_convert_fusion = bf16[24,128,128]{2,0,1:T(8,128)(2,1)S(1)} fusion(f32[24,128,128]{2,0,1:T(8,128)} %fusion.4, f32[24,128,128]{2,0,1:T(8,128)} %fusion.6, f32[24,128,128]{2,0,1:T(8,128)} %fusion.8, f32[24,128,128]{2,0,1:T(8,128)} %fusion.10, f32[24,128,128]{2,0,1:T(8,128)} %fusion.12, f32[24,128,128]{2,0,1:T(8,128)S(1)} %fusion.16, ...), kind=kOutput, calls=%fused_computation.12 | convolution fusion | flops 78643968 | bytes 12845136 | tf_op jit(solution)/shard_map/rk,ktf->rtf/dot_general | solution.py:47
  102.0 0.2 copy.8
  102.2 1.6 %collective-permute-start.7 = (bf16[3072,128]{1,0:T(8,128)(2,1)S(1)}, bf16[3072,128]{1,0:T(8,128)(2,1)S(1)}, u32[]{:S(2)}, u32[]{:S(2)}) collective-permute-start(bf16[3072,128]{1,0:T(8,128)(2,1)S(1)} %bitcast.65), channel_id=1, source_target_pairs={{0,1},{1,2},{2,3},{3,0},{4,5},{5,6},{6,7},{7,4},{8,9},{9,10},{10,1... | collective-permute-start | bytes 2359304 | tf_op jit(solution)/shard_map/ppermute | solution.py:14
  103.8 19.8 %collective-permute-done.7 = bf16[3072,128]{1,0:T(8,128)(2,1)S(1)} collective-permute-done((bf16[3072,128]{1,0:T(8,128)(2,1)S(1)}, bf16[3072,128]{1,0:T(8,128)(2,1)S(1)}, u32[]{:S(2)}, u32[]{:S(2)}) %collective-permute-start.7) | collective-permute-done | bytes 786464 | tf_op jit(solution)/shard_map/ppermute | solution.py:14
  123.6 3.8 %collective-permute-start.9 = (bf16[3072,128]{1,0:T(8,128)(2,1)S(1)}, bf16[3072,128]{1,0:T(8,128)(2,1)S(1)}, u32[]{:S(2)}, u32[]{:S(2)}) collective-permute-start(bf16[3072,128]{1,0:T(8,128)(2,1)S(1)} %bitcast.66), channel_id=1, source_target_pairs={{0,3},{1,0},{2,1},{3,2},{4,7},{5,4},{6,5},{7,6},{8,11},{9,8},{10,9... | collective-permute-start | bytes 2359304 | tf_op jit(solution)/shard_map/ppermute | solution.py:17
  127.4 18.5 %collective-permute-done.8 = bf16[3072,128]{1,0:T(8,128)(2,1)S(1)} collective-permute-done((bf16[3072,128]{1,0:T(8,128)(2,1)S(1)}, bf16[3072,128]{1,0:T(8,128)(2,1)S(1)}, u32[]{:S(2)}, u32[]{:S(2)}) %collective-permute-start.8) | collective-permute-done | bytes 786464 | tf_op jit(solution)/shard_map/ppermute | solution.py:14
  145.9 0.2 constant_dynamic-update-slice_fusion.7
  146.1 0.3 constant_dynamic-update-slice_fusion.6
  146.4 0.3 constant_dynamic-update-slice_fusion.5
  146.7 12.5 %collective-permute-done.9 = bf16[3072,128]{1,0:T(8,128)(2,1)S(1)} collective-permute-done((bf16[3072,128]{1,0:T(8,128)(2,1)S(1)}, bf16[3072,128]{1,0:T(8,128)(2,1)S(1)}, u32[]{:S(2)}, u32[]{:S(2)}) %collective-permute-start.9) | collective-permute-done | bytes 786464 | tf_op jit(solution)/shard_map/ppermute | solution.py:17
  159.2 0.3 constant_dynamic-update-slice_fusion.4
  159.4 0.3 constant_dynamic-update-slice_fusion.3
  159.7 0.3 constant_dynamic-update-slice_fusion.2
  160.0 0.3 constant_dynamic-update-slice_fusion.1
  160.3 0.3 constant_dynamic-update-slice_fusion
  160.6 1.9 %fusion.1 = bf16[3072,128]{1,0:T(8,128)(2,1)} fusion(bf16[3072,1024]{1,0:T(8,128)(2,1)S(1)} %constant_dynamic-update-slice_fusion, s32[]{:T(128)S(6)} %select_n.24, f32[128]{0:T(128)S(1)} %copy-done.3, bf16[512,512]{1,0:T(8,128)(2,1)S(1)} %copy-done, s32[]{:T(128)S(6)} %select_n.25), kind=kOutput, calls=%fused_computation.10 | convolution fusion | flops 403832832 | bytes 4063752 | tf_op jit(solution)/shard_map/dot_general | solution.py:71
  (25 shorter events, 0.2 us)
Async XLA Ops:
  0.0 160.5 %copy-start = (bf16[512,512]{1,0:T(8,128)(2,1)S(1)}, bf16[512,512]{1,0:T(8,128)(2,1)}, u32[]{:S(2)}) copy-start(bf16[512,512]{1,0:T(8,128)(2,1)} %param.14) | copy-start | bytes 1572868
  0.0 26.8 %copy-start.2 = (s32[128]{0:T(128)S(1)}, s32[128]{0:T(128)}, u32[]{:S(2)}) copy-start(s32[128]{0:T(128)} %param.11) | copy-start | bytes 1540
  0.0 13.2 %collective-permute-start = (bf16[3072,128]{1,0:T(8,128)(2,1)}, bf16[3072,128]{1,0:T(8,128)(2,1)S(1)}, u32[]{:S(2)}, u32[]{:S(2)}) collective-permute-start(bf16[3072,128]{1,0:T(8,128)(2,1)} %param.9), channel_id=1, source_target_pairs={{0,4},{4,8},{8,12},{12,16},{16,20},{20,24},{24,28},{28,0},{1,5},{5... | collective-permute-start | bytes 2359304 | tf_op jit(solution)/shard_map/ppermute | solution.py:29
  13.2 12.4 %copy-start.1 = (bf16[3072,128]{1,0:T(8,128)(2,1)}, bf16[3072,128]{1,0:T(8,128)(2,1)S(1)}, u32[]{:S(2)}) copy-start(bf16[3072,128]{1,0:T(8,128)(2,1)S(1)} %collective-permute-done) | copy-start | bytes 2359300
  13.2 12.4 %collective-permute-start.1 = (bf16[3072,128]{1,0:T(8,128)(2,1)S(1)}, bf16[3072,128]{1,0:T(8,128)(2,1)}, u32[]{:S(2)}, u32[]{:S(2)}) collective-permute-start(bf16[3072,128]{1,0:T(8,128)(2,1)S(1)} %collective-permute-done), channel_id=1, source_target_pairs={{0,4},{4,8},{8,12},{12,16},{16,20},{20,24},{24,28},{28,0},{1,5},{5... | collective-permute-start | bytes 2359304 | tf_op jit(solution)/shard_map/ppermute | solution.py:29
  25.6 12.6 %collective-permute-start.2 = (bf16[3072,128]{1,0:T(8,128)(2,1)}, bf16[3072,128]{1,0:T(8,128)(2,1)}, u32[]{:S(2)}, u32[]{:S(2)}) collective-permute-start(bf16[3072,128]{1,0:T(8,128)(2,1)} %collective-permute-done.1), channel_id=1, source_target_pairs={{0,4},{4,8},{8,12},{12,16},{16,20},{20,24},{24,28},{28,0},{1,5},{5... | collective-permute-start | bytes 2359304 | tf_op jit(solution)/shard_map/ppermute | solution.py:29
  38.3 12.8 %collective-permute-start.3 = (bf16[3072,128]{1,0:T(8,128)(2,1)}, bf16[3072,128]{1,0:T(8,128)(2,1)}, u32[]{:S(2)}, u32[]{:S(2)}) collective-permute-start(bf16[3072,128]{1,0:T(8,128)(2,1)} %collective-permute-done.2), channel_id=1, source_target_pairs={{0,4},{4,8},{8,12},{12,16},{16,20},{20,24},{24,28},{28,0},{1,5},{5... | collective-permute-start | bytes 2359304 | tf_op jit(solution)/shard_map/ppermute | solution.py:29
  51.0 12.7 %collective-permute-start.4 = (bf16[3072,128]{1,0:T(8,128)(2,1)}, bf16[3072,128]{1,0:T(8,128)(2,1)}, u32[]{:S(2)}, u32[]{:S(2)}) collective-permute-start(bf16[3072,128]{1,0:T(8,128)(2,1)} %collective-permute-done.3), channel_id=1, source_target_pairs={{0,4},{4,8},{8,12},{12,16},{16,20},{20,24},{24,28},{28,0},{1,5},{5... | collective-permute-start | bytes 2359304 | tf_op jit(solution)/shard_map/ppermute | solution.py:29
  63.7 13.0 %collective-permute-start.5 = (bf16[3072,128]{1,0:T(8,128)(2,1)}, bf16[3072,128]{1,0:T(8,128)(2,1)}, u32[]{:S(2)}, u32[]{:S(2)}) collective-permute-start(bf16[3072,128]{1,0:T(8,128)(2,1)} %collective-permute-done.4), channel_id=1, source_target_pairs={{0,4},{4,8},{8,12},{12,16},{16,20},{20,24},{24,28},{28,0},{1,5},{5... | collective-permute-start | bytes 2359304 | tf_op jit(solution)/shard_map/ppermute | solution.py:29
  76.7 14.1 %collective-permute-start.6 = (bf16[3072,128]{1,0:T(8,128)(2,1)}, bf16[3072,128]{1,0:T(8,128)(2,1)}, u32[]{:S(2)}, u32[]{:S(2)}) collective-permute-start(bf16[3072,128]{1,0:T(8,128)(2,1)} %collective-permute-done.5), channel_id=1, source_target_pairs={{0,4},{4,8},{8,12},{12,16},{16,20},{20,24},{24,28},{28,0},{1,5},{5... | collective-permute-start | bytes 2359304 | tf_op jit(solution)/shard_map/ppermute | solution.py:29
  102.2 21.4 %collective-permute-start.7 = (bf16[3072,128]{1,0:T(8,128)(2,1)S(1)}, bf16[3072,128]{1,0:T(8,128)(2,1)S(1)}, u32[]{:S(2)}, u32[]{:S(2)}) collective-permute-start(bf16[3072,128]{1,0:T(8,128)(2,1)S(1)} %bitcast.65), channel_id=1, source_target_pairs={{0,1},{1,2},{2,3},{3,0},{4,5},{5,6},{6,7},{7,4},{8,9},{9,10},{10,1... | collective-permute-start | bytes 2359304 | tf_op jit(solution)/shard_map/ppermute | solution.py:14
  123.6 22.3 %collective-permute-start.8 = (bf16[3072,128]{1,0:T(8,128)(2,1)S(1)}, bf16[3072,128]{1,0:T(8,128)(2,1)S(1)}, u32[]{:S(2)}, u32[]{:S(2)}) collective-permute-start(bf16[3072,128]{1,0:T(8,128)(2,1)S(1)} %collective-permute-done.7), channel_id=1, source_target_pairs={{0,1},{1,2},{2,3},{3,0},{4,5},{5,6},{6,7},{7,4},{8,9},{9,10},{10,1... | collective-permute-start | bytes 2359304 | tf_op jit(solution)/shard_map/ppermute | solution.py:14
  123.6 35.6 %collective-permute-start.9 = (bf16[3072,128]{1,0:T(8,128)(2,1)S(1)}, bf16[3072,128]{1,0:T(8,128)(2,1)S(1)}, u32[]{:S(2)}, u32[]{:S(2)}) collective-permute-start(bf16[3072,128]{1,0:T(8,128)(2,1)S(1)} %bitcast.66), channel_id=1, source_target_pairs={{0,3},{1,0},{2,1},{3,2},{4,7},{5,4},{6,5},{7,6},{8,11},{9,8},{10,9... | collective-permute-start | bytes 2359304 | tf_op jit(solution)/shard_map/ppermute | solution.py:17
  146.7 13.9 %copy-start.3 = (f32[128]{0:T(128)S(1)}, f32[128]{0:T(128)}, u32[]{:S(2)}) copy-start(f32[128]{0:T(128)} %param.15) | copy-start | bytes 1540
